TPU v7x, 256 devices: a whole 4x4x8 slice. The times are simulated.
256 devices in a mesh: seq: 16 (over x_hi, y, core), head: 16 (over x_lo, z).
Axes of the slice: x: 4 (x_hi: 2, x_lo: 2; x = x_hi * 2 + x_lo), y: 4, z: 8, core: 2. Of those that a mesh axis runs over, the one named last changes fastest.
Arguments:
- grad_out: bfloat16 [4096, 8192], P('seq', 'head'), may hold values from -6 to 6
- out_weight: bfloat16 [16384, 8192], P('head', 'seq'), may hold values from -0.046875 to 0.046875
- ssm_input: bfloat16 [4096, 16384], P('seq', 'head'), may hold values from -6 to 6
- step_size: float32 [4096, 128], P('seq', 'head'), may hold values from 0.02 to 0.2
- log_decay: float32 [4096, 128], P('seq', 'head'), may hold values from -1 to 0, as said below
- b_in: bfloat16 [4096, 256], P('seq'), may hold values from -1.5 to 1.5
- c_in: bfloat16 [4096, 256], P('seq'), may hold values from -1.5 to 1.5
- skip: float32 [128], P('head'), may hold values from 0.5 to 1.5
Outputs:
- grad_input: bfloat16 [4096, 16384], P('seq', 'head')
- grad_step: float32 [4096, 128], P('seq', 'head')
- grad_decay: float32 [4096, 128], P('seq', 'head')
- grad_b: float32 [4096, 256], P('seq')
- grad_c: float32 [4096, 256], P('seq')
Inputs may be any that keep to these rules, and one draw needn't show every extreme that they name: `log_decay`: every entry is negative.
All inputs are finite; a program needn't handle non-finite values.
Results may differ from a plain program's by a relative error of at most 0.0049.
Values may be sent and summed in bfloat16 or wider, within the bound.
A program may use at most 64 MiB of HBM per device.

v0:
```python
import jax
import jax.numpy as jnp
from jax import lax
from jax.sharding import PartitionSpec as P

HIGH = lax.Precision.HIGHEST


def entering(part, axis, combine, identity, reverse):
    count = lax.axis_size(axis)
    place = lax.axis_index(axis)
    ahead = count - 1 - place if reverse else place
    gathered = jax.tree.map(lambda a: lax.all_gather(a, axis), part)
    state = jax.tree.map(lambda a, e: jnp.zeros_like(a) + jnp.asarray(e, a.dtype), part, identity)

    def one(hop, state):
        source = count - 1 - hop if reverse else hop
        return combine(
            state, jax.tree.map(lambda a: lax.dynamic_index_in_dim(a, source, 0, False), gathered)
        )

    return lax.fori_loop(0, ahead, one, state)


def inner_terms(inputs, strides, running, b_rows, c_rows, skips):
    span = inputs.shape[0]
    row_pos = lax.broadcasted_iota(jnp.int32, (span, span), 0)
    col_pos = lax.broadcasted_iota(jnp.int32, (span, span), 1)
    causal = row_pos >= col_pos
    running_t = running.T
    gaps = running_t[:, :, None] - running_t[:, None, :]
    weights = jnp.exp(jnp.where(causal[None], gaps, -jnp.inf)) * strides.T[:, None, :]
    intersection = jnp.dot(c_rows, b_rows.T, precision=HIGH)
    mixed_sum = jnp.einsum("hts,shp->thp", weights * intersection[None], inputs, precision=HIGH)
    return mixed_sum + skips[None, :, None] * inputs


def carried(c_rows, running, carried_state):
    readout = jnp.einsum("tn,hpn->thp", c_rows, carried_state, precision=HIGH)
    return readout * jnp.exp(running)[:, :, None]


def closing(inputs, strides, b_rows, running, carried_state):
    block_end = running[-1]
    input_scale = strides * jnp.exp(block_end[None, :] - running)
    fresh = jnp.einsum("thp,tn->hpn", inputs * input_scale[:, :, None], b_rows, precision=HIGH)
    return jnp.exp(block_end)[:, None, None] * carried_state + fresh


def block_forward(inputs, strides, decays, b_rows, c_rows, skips, carried_state):
    running = jnp.cumsum(decays, axis=0)
    outputs = inner_terms(inputs, strides, running, b_rows, c_rows, skips) + carried(
        c_rows, running, carried_state
    )
    return (outputs, closing(inputs, strides, b_rows, running, carried_state))


def compose(first_part, second_part):
    return (
        first_part[0] * second_part[0],
        second_part[0][:, None, None] * first_part[1] + second_part[1],
    )


def local(grad_out, out_weight, ssm_input, step_size, log_decay, b_in, c_in, skip):
    full_grad = lax.all_gather(grad_out, "head", axis=1, tiled=True)
    span = ssm_input.shape[0]
    head_count = step_size.shape[1]
    head_width = ssm_input.shape[1] // head_count
    state_count = b_in.shape[1]
    grad_y = lax.dot_general(
        full_grad,
        lax.all_gather(out_weight, "seq", axis=1, tiled=True),
        (((1,), (1,)), ((), ())),
        preferred_element_type=jnp.float32,
    ).astype(jnp.bfloat16)
    inputs = ssm_input.astype(jnp.float32).reshape(span, head_count, head_width)
    upstream = grad_y.astype(jnp.float32).reshape(span, head_count, head_width)
    b_float = b_in.astype(jnp.float32)
    c_float = c_in.astype(jnp.float32)
    zero_state = jnp.zeros((head_count, head_width, state_count), jnp.float32)
    running = jnp.cumsum(log_decay, axis=0)
    block_decay = jnp.exp(running[-1])
    local_states = closing(inputs, step_size, b_float, running, zero_state)
    local_grads = jnp.einsum(
        "thp,tn->hpn", upstream * jnp.exp(running)[:, :, None], c_float, precision=HIGH
    )
    identity = (jnp.ones((head_count,), jnp.float32), jnp.zeros_like(zero_state))
    incoming = entering((block_decay, local_states), "seq", compose, identity, False)[1]
    outgoing = entering((block_decay, local_grads), "seq", compose, identity, True)[1]

    def forward_full(inputs_v, strides_v, decays_v, b_rows, c_rows):
        return block_forward(inputs_v, strides_v, decays_v, b_rows, c_rows, skip, incoming)

    pull_full = jax.vjp(forward_full, inputs, step_size, log_decay, b_float, c_float)[1]
    gradients = pull_full((upstream, outgoing))
    grad_b, grad_c = lax.psum((gradients[3], gradients[4]), "head")
    grad_input = gradients[0].reshape(span, head_count * head_width).astype(jnp.bfloat16)
    return (grad_input, gradients[1], gradients[2], grad_b, grad_c)


def solution(mesh):
    in_specs = (
        P("seq", "head"),
        P("head", "seq"),
        P("seq", "head"),
        P("seq", "head"),
        P("seq", "head"),
        P("seq", None),
        P("seq", None),
        P("head"),
    )
    out_specs = (
        P("seq", "head"),
        P("seq", "head"),
        P("seq", "head"),
        P("seq", None),
        P("seq", None),
    )
    return jax.shard_map(local, mesh=mesh, in_specs=in_specs, out_specs=out_specs, check_vma=False)
```

profile of v0, /device:TPU:1, one launch (start us, length us, event | category | flops | bytes accessed | tf_op | source)
XLA Modules:
  0.0 639.5 jit_solution(1202185131992663605)
XLA Ops:
  7.2 0.7 all-gather.8.cloned.1.call-update
  8.0 0.7 all-gather.10.cloned.1.call-update
  8.7 0.0 all-gather.12.cloned.1.call-start
  8.7 1.3 reduce-window.14
  10.0 0.2 slice_reduce_fusion.1
  10.2 0.1 fusion.45
  10.2 71.5 %all-gather.8.cloned.1.call-done = bf16[256,8192]{1,0:T(8,128)(2,1)} async-done(((bf16[256,512]{1,0:T(8,128)(2,1)}), bf16[256,8192]{1,0:T(8,128)(2,1)}) %all-gather.8.cloned.1.call-update) | async-done | bytes 4194320 | tf_op jit(solution)/shard_map/all_gather | solution.py:66
  81.7 133.3 %all-gather.10.cloned.1.call-done = bf16[1024,8192]{1,0:T(8,128)(2,1)} async-done(((bf16[1024,512]{1,0:T(8,128)(2,1)}), bf16[1024,8192]{1,0:T(8,128)(2,1)}) %all-gather.10.cloned.1.call-update) | async-done | bytes 16777232 | tf_op jit(solution)/shard_map/all_gather | solution.py:73
  215.0 11.6 %convolution_convert_fusion = bf16[256,1024]{1,0:T(8,128)(2,1)S(1)} fusion(bf16[256,8192]{1,0:T(8,128)(2,1)} %all-gather.8.cloned.1.call-done, bf16[1024,8192]{1,0:T(8,128)(2,1)} %all-gather.10.cloned.1.call-done), kind=kOutput, calls=%fused_computation.22 | convolution fusion | flops 4295229440 | bytes 21495808 | tf_op jit(solution)/shard_map/dot_general | solution.py:71
  226.5 0.1 copy.80
  226.7 0.3 copy.59
  227.0 0.4 copy-done.1
  227.4 1.7 fusion.15
  229.1 0.0 all-gather.14.cloned.1.call-start
  229.2 0.2 copy.63
  229.4 0.2 slice_reduce_fusion.2
  229.6 19.7 %all-gather.2 = f32[16,1,8]{2,1,0:T(1,128)S(1)} all-gather(f32[1,1,8]{2,1,0:T(1,128)S(1)} %bitcast.129), channel_id=1, replica_groups=mesh['seq'=16,'head'=16] {'seq'}, dimensions={0}, use_global_device_ids=true | all-gather | bytes 544 | tf_op jit(solution)/shard_map/all_gather | solution.py:13
  249.3 0.5 exponential_multiply_fusion
  249.8 0.1 add_bitcast_fusion.2
  249.9 0.2 fusion.46
  250.1 1.6 fusion.18
  251.8 89.1 %all-gather.12.cloned.1.call-done = f32[128,128,256]{2,1,0:T(8,128)} async-done(((f32[8,128,256]{2,1,0:T(8,128)}), f32[128,128,256]{2,1,0:T(8,128)}) %all-gather.12.cloned.1.call-update) | async-done | bytes 16777232 | tf_op jit(solution)/shard_map/all_gather | solution.py:13
  340.8 0.1 broadcast.25.clone
  340.9 22.1 %while.26 = (s32[]{:T(128)}, f32[8,128,256]{2,1,0:T(8,128)S(1)}, s32[]{:T(128)}, f32[16,8]{1,0:T(8,128)S(1)}, f32[16,8,128,256]{3,2,1,0:T(8,128)}, /*index=5*/s32[]{:T(128)}, s32[]{:T(128)}, s32[]{:T(128)}, s32[]{:T(128)}) while((s32[]{:T(128)}, f32[8,128,256]{2,1,0:T(8,128)S(1)}, s32[]{:T(128)}, f32[16,8]{1,0:T(8,128)S(1)}, ...), condition=%wide.region_3.4_spmd, body=%wide.region_2.3_spmd.sunk | while | flops 524294 | bytes 3145979 | solution.py:22
  341.0 1.5 bitcast_add_fusion.6
  342.6 1.5 bitcast_add_fusion.6
  344.1 1.5 bitcast_add_fusion.6
  345.7 1.5 bitcast_add_fusion.6
  347.3 1.5 bitcast_add_fusion.6
  348.9 1.5 bitcast_add_fusion.6
  350.4 1.5 bitcast_add_fusion.6
  352.0 1.5 bitcast_add_fusion.6
  353.6 1.5 bitcast_add_fusion.6
  355.2 1.5 bitcast_add_fusion.6
  356.7 1.5 bitcast_add_fusion.6
  358.3 1.5 bitcast_add_fusion.6
  359.9 1.5 bitcast_add_fusion.6
  361.5 1.5 bitcast_add_fusion.6
  363.0 1.7 fusion.21
  364.7 1.3 fusion.44
  366.0 1.7 convolution_add_fusion
  367.7 0.2 all-reduce.4.cloned.1.call-start
  367.9 3.8 fusion.10
  371.7 2.0 copy.70
  373.7 0.1 copy.67
  373.8 1.8 fusion.20
  375.6 1.1 convolution_add_fusion.2
  376.7 103.4 %all-gather.14.cloned.1.call-done = f32[128,128,256]{2,1,0:T(8,128)} async-done(((f32[8,128,256]{2,1,0:T(8,128)}), f32[128,128,256]{2,1,0:T(8,128)}) %all-gather.14.cloned.1.call-update) | async-done | bytes 16777232 | tf_op jit(solution)/shard_map/all_gather | solution.py:13
  480.1 0.1 broadcast.25
  480.2 1.6 while.27
  480.2 1.5 bitcast_add_fusion.7
  481.8 0.2 multiply_reduce_fusion.2
  482.0 0.6 fusion.16
  482.6 1.8 fusion.19
  484.5 0.1 copy.66
  484.5 1.0 convolution_add_fusion.1
  485.5 0.1 multiply_add_fusion
  485.6 0.1 fusion.40
  485.7 2.5 reduce-window.16
  488.2 0.1 slice_reduce_fusion
  488.3 0.7 add_bitcast_fusion
  489.0 140.7 %all-reduce.4.cloned.1.call-done = (f32[256,256]{1,0:T(8,128)}, f32[256,256]{1,0:T(8,128)}) async-done(((f32[256,256]{1,0:T(8,128)}, f32[256,256]{1,0:T(8,128)}), (f32[256,256]{1,0:T(8,128)}, f32[256,256]{1,0:T(8,128)})) %all-reduce.4.cloned.1.call-update) | async-done | bytes 524304 | tf_op jit(solution)/shard_map/psum | solution.py:97
  629.7 1.7 copy.107
  631.3 1.7 copy.108
  (40 shorter events, 0.4 us)
Async XLA Ops:
  7.2 242.7 %copy-start = (bf16[256,256]{1,0:T(8,128)(2,1)S(1)}, bf16[256,256]{1,0:T(8,128)(2,1)}, u32[]{:S(2)}) copy-start(bf16[256,256]{1,0:T(8,128)(2,1)} %param.17) | copy-start | bytes 393220
  7.2 74.5 %all-gather.8.cloned.1.call-start = ((), (), s32[]{:S(2)}) async-start(), calls=%async_computation | async-start | bytes 4456448 | tf_op jit(solution)/shard_map/all_gather | solution.py:66
  7.9 207.0 %all-gather.10.cloned.1.call-start = ((), (), s32[]{:S(2)}) async-start(), calls=%async_computation.1 | async-start | bytes 17825792 | tf_op jit(solution)/shard_map/all_gather | solution.py:73
  8.7 332.2 %all-gather.12.cloned.1.call-start = ((), (), s32[]{:S(2)}) async-start(), calls=%async_computation.2 | async-start | bytes 17825792 | tf_op jit(solution)/shard_map/all_gather | solution.py:13
  226.5 0.9 copy-start.1
  226.6 2.5 copy-start.2
  227.4 22.7 %copy-start.3 = (f32[256,8]{0,1:T(8,128)S(1)}, f32[256,8]{0,1:T(8,128)}, u32[]{:S(2)}) copy-start(f32[256,8]{0,1:T(8,128)} %param.15) | copy-start | bytes 24580
  229.1 251.0 %all-gather.14.cloned.1.call-start = ((), (), s32[]{:S(2)}) async-start(), calls=%async_computation.3 | async-start | bytes 17825792 | tf_op jit(solution)/shard_map/all_gather | solution.py:13
  229.6 22.2 %copy-start.4 = (f32[8]{0:T(128)}, f32[8]{0:T(128)S(1)}, u32[]{:S(2)}) copy-start(f32[8]{0:T(128)S(1)} %get-tuple-element.199) | copy-start | bytes 100
  363.0 1.7 copy-start.5
  363.0 3.0 copy-start.7
  367.7 262.0 %all-reduce.4.cloned.1.call-start = ((), (), s32[]{:S(2)}) async-start(), calls=%async_computation.4 | async-start | bytes 1048576 | tf_op jit(solution)/shard_map/psum | solution.py:97
  367.9 5.8 copy-start.6
Sparse Core Ops, SparseCore 0:
  9.8 71.8 all-gather.7
  84.3 130.6 all-gather.9
  229.2 111.5 all-gather.11
  367.8 112.2 all-gather.13
  485.7 143.8 all-reduce.3
where the time goes:
time: 650 us; the launch traced here: 640 us
  waiting for transfers between devices  539 us (83%)
  other arithmetic  29.9 us (5%)
  matrix products  28.5 us (4%)
  blocking collectives  19.7 us (3%)
  between operations  14 us (2%)
  local copies, waits for them, and re-layouts  7.42 us (1%)
    all_gather x2, waiting for transfers between devices, entering(): gathered = jax.tree.map(lambda a: lax.all_gather(a, axis), part)  192 us
    psum x1, waiting for transfers between devices, local(): grad_b, grad_c = lax.psum((gradients[3], gradients[4]), 'head')  141 us
    all_gather x1, waiting for transfers between devices, local(): lax.all_gather(out_weight, 'seq', axis=1, tiled=True)  133 us
    all_gather x1, waiting for transfers between devices, local(): full_grad = lax.all_gather(grad_out, 'head', axis=1, tiled=True)  71.5 us
    add x15, other arithmetic, compose(): second_part[0][:, None, None] * first_part[1] + second_part[1]  23 us
    all_gather x1, blocking collectives, entering(): gathered = jax.tree.map(lambda a: lax.all_gather(a, axis), part)  19.7 us
  transfers between devices with their start and end apart: 5, of which 5 were waited for; matrix products, arithmetic and copies ran while one was open for 3% of the time, Pallas kernels for 0%

commit v1 on v0

v1 whole, which is shorter than its diff:
```python
import jax
import jax.numpy as jnp
from jax import lax
from jax.experimental import pallas as pl
from jax.experimental.pallas import tpu as pltpu
from jax.sharding import PartitionSpec as P

F32, BF16 = jnp.float32, jnp.bfloat16
HIGH = lax.Precision.HIGHEST
NN = (((1,), (0,)), ((), ()))
NT = (((1,), (1,)), ((), ()))
TN = (((0,), (0,)), ((), ()))

TOK = 256
HEADS = 8
WIDTH = 128
STATE = 256
ROWS = HEADS * WIDTH
COLS = 512
GROUP = 16
SLICE = ROWS // GROUP
PART = TOK // GROUP
CUT = 608


def mm(a, b, dims):
    return lax.dot_general(a, b, dims, preferred_element_type=F32)


def exact(a, b, dims):
    return lax.dot_general(a, b, dims, precision=HIGH, preferred_element_type=F32)


def split(a):
    high = a.astype(BF16)
    return high, (a - high.astype(F32)).astype(BF16)


def remote(src, dst, send_sem, recv_sem, seq, head):
    return pltpu.make_async_remote_copy(
        src_ref=src,
        dst_ref=dst,
        send_sem=send_sem,
        recv_sem=recv_sem,
        device_id={"seq": seq, "head": head},
        device_id_type=pl.DeviceIdType.MESH,
    )


LOW, TOP = (0, CUT), (CUT, ROWS)
LOW0, LOW1 = (0, CUT // 2), (CUT // 2, CUT)
TOP0, TOP1 = (CUT, (CUT + ROWS) // 2), ((CUT + ROWS) // 2, ROWS)
HOPS = {
    "b1": (0, 0, TOP, "up"),
    "b2": (0, 0, TOP, "down"),
    "b0": (0, 0, TOP, "x"),
    "a1": (0, 0, LOW, "up"),
    "a2": (0, 0, LOW, "down"),
    "a0": (0, 0, LOW, "x"),
    "b5": (0, -1, TOP0, "up"),
    "b7": (0, -1, TOP, "x"),
    "b6": (0, 1, TOP1, "down"),
    "b8": (0, 1, TOP, "x"),
    "b9": (0, 2, TOP0, "x"),
    "b10": (0, 2, TOP1, "x"),
    "a5": (0, -1, LOW0, "up"),
    "a6": (0, 1, LOW1, "down"),
    "a3": (1, 0, LOW, "up"),
    "a4": (1, 0, LOW, "down"),
    "a7": (1, -1, LOW0, "up"),
    "a8": (1, 1, LOW1, "down"),
}
HOP_AT = {name: at for at, name in enumerate(HOPS)}


def kernel(
    go_ref, w_ref, x_ref, dt_ref, ld_ref, b_ref, c_ref, skip_ref,
    gi_ref, gs_ref, gd_ref, gb_ref, gc_ref,
    wbuf, gbuf, acc, pbuf, gy, ge, xs, dxs, cb, vsum, urow, dcol, qcol, dtile, decs,
    sfw, rfw, ofw, hbuf, sbw, rbw, obw, qbuf, dcp, dbp, prc, prb, gcs, gbs,
    w_s, w_r, g_s, g_r, z_s, z_r, p_s, p_r, e_s, e_r, f_s, f_r, h_s, h_r, l_s, l_r, q_s, q_r,
    rc_s, rc_r, ac_s, ac_r, rb_s, rb_r, ab_s, ab_r,
):
    seq = lax.axis_index("seq")
    head = lax.axis_index("head")
    xh = lax.div(seq, 8)
    yy = lax.rem(lax.div(seq, 2), 4)
    core = lax.rem(seq, 2)
    xl = lax.div(head, 8)
    zz = lax.rem(head, 8)
    other = seq + 1 - 2 * core
    beside = (1 - xl) * 8 + zz
    home = lax.rem(zz, 2)
    odd = lax.rem(zz + core, 2)

    barrier = pltpu.get_barrier_semaphore()

    def greet(s, h):
        pl.semaphore_signal(
            barrier, inc=1, device_id={"seq": s, "head": h}, device_id_type=pl.DeviceIdType.MESH
        )

    for d in range(1, GROUP):
        greet(lax.rem(seq + d, GROUP), head)
        greet(seq, lax.rem(head + d, GROUP))
    greet(other, beside)
    pl.semaphore_wait(barrier, 2 * (GROUP - 1) + 1)

    sent = []

    def start(copy):
        copy.start()
        sent.append(copy)

    def shard(dx, dy):
        x_at = xh if dx == 0 else 1 - xh
        return x_at * 4 + lax.rem(yy + dy + 4, 4)

    def hop(name):
        dx, dy, (lo, hi), way = HOPS[name]
        at = HOP_AT[name]
        where = pl.ds(lo, hi - lo)
        slot = wbuf.at[shard(dx, dy), where]
        src = w_ref.at[where] if (dx, dy) == (0, 0) else slot
        if way == "x":
            to = (1 - xh) * 8 + yy * 2 + core
        else:
            to = xh * 8 + lax.rem(yy + (1 if way == "up" else 3), 4) * 2 + core
        return remote(src, slot, w_s.at[at], w_r.at[at], to, head)

    def go(*names):
        for name in names:
            start(hop(name))

    def got(*names):
        for name in names:
            dx, dy, (lo, hi), way = HOPS[name]
            at = HOP_AT[name]
            if way == "x":
                dx = 1 - dx
            else:
                dy = dy - 1 if way == "up" else dy + 1
            slot = wbuf.at[shard(dx, dy), pl.ds(lo, hi - lo)]
            remote(slot, slot, w_s.at[at], w_r.at[at], seq, head).wait_recv()

    home_seq = seq - core + home
    own_at = xl * 4 + lax.div(zz, 2)
    beside_at = (1 - xl) * 4 + lax.div(zz, 2)
    across = remote(go_ref, gbuf.at[own_at, core], g_s.at[0], g_r.at[core], home_seq, beside)
    start(across)
    to_other = remote(go_ref, gbuf.at[own_at, core], g_s.at[1], g_r.at[2], other, head)

    @pl.when(odd == 1)
    def _():
        to_other.start()

    go("b1", "b2", "b0", "a1", "a2", "a0")

    @pl.when(odd == 0)
    def _():
        gbuf[own_at, core] = go_ref[...]

    def unit(x_at, way, d, half):
        z_from = lax.rem(zz + (8 - d if way == 0 else d), 8)
        k = x_at * 4 + lax.div(z_from, 2)
        return gbuf.at[k, way] if half else gbuf.at[k]

    def z_hop(way, stage, x_at, is_odd):
        part = unit(x_at, way, 2 * stage + is_odd, is_odd and stage == 1)
        z_to = lax.rem(zz + (1 if way == 0 else 7), 8)
        return remote(
            part, part, z_s.at[way, stage, x_at], z_r.at[way, stage, x_at], seq, xl * 8 + z_to
        )

    def z_got(way, stage, x_at, is_odd):
        part = unit(x_at, way, 2 * stage + (1 if is_odd else 2), (not is_odd) and stage == 1)
        remote(
            part, part, z_s.at[way, stage, x_at], z_r.at[way, stage, x_at], seq, head
        ).wait_recv()

    pairs = [(way, x_at) for x_at in range(2) for way in range(2)]

    def z_start(stage, is_odd):
        for way, x_at in pairs:
            z_hop(way, stage, x_at, is_odd).start()

    def z_pass(stage_in, stage_out, is_odd):
        for way, x_at in pairs:
            z_got(way, stage_in, x_at, is_odd)
            if stage_out is not None:
                z_hop(way, stage_out, x_at, is_odd).start()

    rows_i = lax.broadcasted_iota(jnp.int32, (TOK, TOK), 0)
    cols_i = lax.broadcasted_iota(jnp.int32, (TOK, TOK), 1)
    causal = rows_i >= cols_i
    lower = jnp.where(causal, 1.0, 0.0).astype(F32)
    upper = jnp.where(rows_i <= cols_i, 1.0, 0.0).astype(F32)
    eye = jnp.where(rows_i == cols_i, 1.0, 0.0).astype(F32)
    lane = lax.broadcasted_iota(jnp.int32, (TOK, HEADS), 1)
    lane1 = lax.broadcasted_iota(jnp.int32, (1, HEADS), 1)
    dt = dt_ref[...]
    ld = ld_ref[...]
    run = exact(lower, ld, NN)
    run_row = exact(ld, upper, TN)
    dt_row = exact(dt, eye, TN)
    end = run[TOK - 1 : TOK, :]
    fade = jnp.exp(end - run)
    scale = dt * fade
    rise = jnp.exp(run)
    exp_end = jnp.exp(end)

    b_all = b_ref[...]
    c_all = c_ref[...]
    for h in range(HEADS):
        ch = slice(h * WIDTH, (h + 1) * WIDTH)
        scaled = x_ref[:, ch].astype(F32) * scale[:, h : h + 1]
        part, rest = split(scaled)
        xs[:, ch] = part
        made = mm(part, b_all, TN) + mm(rest, b_all, TN)
        sfw[2 * h : 2 * h + 2] = made.reshape(2, SLICE, STATE)
        dtile[h] = jnp.broadcast_to(exp_end[:, h : h + 1], (8, 128))

    def to_seq(src, dst, ss, rs):
        for d in range(1, GROUP):
            peer = lax.rem(seq + d, GROUP)
            start(remote(src.at[peer], dst.at[seq], ss.at[d], rs.at[d], peer, head))
        dst[seq] = src[seq]

    def from_seq(dst, ss, rs):
        for d in range(1, GROUP):
            peer = lax.rem(seq + GROUP - d, GROUP)
            remote(dst.at[peer], dst.at[peer], ss.at[d], rs.at[d], seq, head).wait_recv()

    for d in range(1, GROUP):
        peer = lax.rem(seq + d, GROUP)
        start(remote(dtile.at[lax.div(peer, 2)], decs.at[seq], e_s.at[d], e_r.at[d], peer, head))
    decs[seq] = dtile[lax.div(seq, 2)]
    to_seq(sfw, rfw, f_s, f_r)

    @pl.when(odd == 0)
    def _():
        for i, at in enumerate((beside_at, beside_at, own_at)):
            tok = i if i < 2 else 1 - core
            slot = gbuf.at[at, tok]
            remote(slot, slot, g_s.at[0], g_r.at[i], seq, head).wait_recv()
        z_start(0, 0)

    cb[...] = mm(c_all, b_all, NT)

    got("b1")
    go("b7", "b5")
    got("b2")
    go("b8", "b6")

    @pl.when(odd == 1)
    def _():
        z_pass(0, 0, 1)

    got("b5")
    go("b9")
    got("b6")
    go("b10")
    got("a1")
    go("a5")
    got("a2")
    go("a6")
    got("a0")
    go("a3", "a4")

    def scan(order, inbox, outbox):
        state = jnp.zeros((SLICE, STATE), F32)
        for s in order:
            outbox[s] = state
            state = state * decs[s, 0:1, 0:1] + inbox[s]

    from_seq(decs, e_s, e_r)
    from_seq(rfw, f_s, f_r)
    scan(range(GROUP), rfw, ofw)
    to_seq(ofw, hbuf, h_s, h_r)

    @pl.when(odd == 0)
    def _():
        z_pass(0, 1, 0)

    got("a3")
    go("a7")
    got("a4")
    go("a8")

    @pl.when(odd == 1)
    def _():
        z_pass(1, 1, 1)

    @pl.when(odd == 0)
    def _():
        z_pass(1, None, 0)

    def block(at, weights, first):
        left = gbuf[at].reshape(2 * TOK, COLS)
        for n in range(4):
            col = slice(n * 256, (n + 1) * 256)
            new = mm(left, weights(n), NT)
            acc[:, col] = new if first else acc[:, col] + new

    def held(dx, dy):
        at = shard(dx, dy)
        return at, lambda n: wbuf[at, n * 256 : (n + 1) * 256, :]

    block(shard(0, 0), lambda n: w_ref[n * 256 : (n + 1) * 256, :], True)
    got("b0")
    block(*held(1, 0), False)
    block(*held(0, -1), False)
    block(*held(0, 1), False)
    got("a5", "a6")
    block(*held(0, 2), False)
    from_seq(hbuf, h_s, h_r)
    got("b7")
    block(*held(1, -1), False)
    got("b8")
    block(*held(1, 1), False)
    got("b9", "b10", "a7", "a8")
    block(*held(1, 2), False)

    mine = pl.ds(pl.multiple_of(core * TOK, TOK), TOK)
    theirs = pl.ds(pl.multiple_of((1 - core) * TOK, TOK), TOK)
    swap = remote(acc.at[theirs], pbuf, p_s.at[0], p_r.at[0], other, head)
    start(swap)
    swap.wait_recv()
    for h in range(HEADS):
        ch = slice(h * WIDTH, (h + 1) * WIDTH)
        up = (acc[mine, ch] + pbuf[:, ch]).astype(BF16)
        gy[:, ch] = up
        part, rest = split(up.astype(F32) * rise[:, h : h + 1])
        ge[:, ch] = part
        made = mm(part, c_all, TN) + mm(rest, c_all, TN)
        sbw[2 * h : 2 * h + 2] = made.reshape(2, SLICE, STATE)
    to_seq(sbw, rbw, l_s, l_r)

    vsum[...] = jnp.zeros((TOK, TOK), F32)
    dcol[...] = jnp.zeros((TOK, HEADS), F32)

    def inner(h):
        ch = slice(h * WIDTH, (h + 1) * WIDTH)
        up = gy[:, ch]
        gx = mm(up, x_ref[:, ch], NT)
        gaps = run[:, h : h + 1] - run_row[h : h + 1, :]
        decay = jnp.exp(jnp.where(causal, gaps, -1e30))
        steps = dt_row[h : h + 1, :]
        mixed = decay * cb[...]
        both = mixed * gx
        vsum[...] += decay * gx * steps
        urow[h : h + 1, :] = jnp.sum(both, axis=0, keepdims=True)
        along = jnp.sum(both * steps, axis=1, keepdims=True)
        dxs[:, ch] = mm((mixed * steps).astype(BF16), up, TN)
        part, rest = split(hbuf[2 * h : 2 * h + 2].reshape(WIDTH, STATE))
        read = mm(c_all, part, NT) + mm(c_all, rest, NT)
        along += rise[:, h : h + 1] * jnp.sum(up.astype(F32) * read, axis=1, keepdims=True)
        dcol[...] += jnp.where(lane == h, along, 0.0)

    for h in range(HEADS // 2):
        inner(h)

    from_seq(rbw, l_s, l_r)
    scan(range(GROUP - 1, -1, -1), rbw, obw)
    to_seq(obw, qbuf, q_s, q_r)

    for h in range(HEADS // 2, HEADS):
        inner(h)

    v_hi = vsum[...].astype(BF16)
    v_lo = (vsum[...] - v_hi.astype(F32)).astype(BF16)

    def spread(src, dst, ss, rs):
        for d in range(1, GROUP):
            peer = lax.rem(head + d, GROUP)
            part = src.at[pl.ds(pl.multiple_of(peer * PART, PART), PART)]
            start(remote(part, dst.at[head], ss.at[d], rs.at[d], seq, peer))
        dst[head] = src[pl.ds(pl.multiple_of(head * PART, PART), PART)]

    def collect(inbox, whole, ss, rs, ss2, rs2):
        for d in range(1, GROUP):
            peer = lax.rem(head + GROUP - d, GROUP)
            remote(inbox.at[peer], inbox.at[peer], ss.at[d], rs.at[d], seq, head).wait_recv()
        total = inbox[0]
        for i in range(1, GROUP):
            total = total + inbox[i]
        own = pl.ds(pl.multiple_of(head * PART, PART), PART)
        whole[own] = total
        for d in range(1, GROUP):
            peer = lax.rem(head + d, GROUP)
            start(remote(whole.at[own], whole.at[own], ss2.at[d], rs2.at[d], seq, peer))

    def finish(whole, out, ss, rs):
        for d in range(1, GROUP):
            peer = lax.rem(head + GROUP - d, GROUP)
            part = whole.at[pl.ds(pl.multiple_of(peer * PART, PART), PART)]
            remote(part, part, ss.at[d], rs.at[d], seq, head).wait_recv()
        out[...] = whole[...]

    dcp[...] = (
        mm(v_hi, b_all, NN)
        + mm(v_lo, b_all, NN)
        + mm(ge[...], hbuf[...].reshape(ROWS, STATE).astype(BF16), NN)
    )
    spread(dcp, prc, rc_s, rc_r)
    dbp[...] = mm(v_hi, c_all, TN) + mm(v_lo, c_all, TN)
    u_col = exact(eye, urow[...], NT)

    from_seq(qbuf, q_s, q_r)
    dbp[...] += mm(xs[...], qbuf[...].reshape(ROWS, STATE).astype(BF16), NN)
    spread(dbp, prb, rb_s, rb_r)
    collect(prc, gcs, rc_s, rc_r, ac_s, ac_r)

    qcol[...] = jnp.zeros((TOK, HEADS), F32)
    inner_hq = jnp.zeros((1, HEADS), F32)
    for h in range(HEADS // 2):
        inner_hq = closing(h, lane, lane1, b_all, x_ref, gy, dxs, hbuf, qbuf, qcol, scale, skip_ref, gi_ref, inner_hq)
    collect(prb, gbs, rb_s, rb_r, ab_s, ab_r)
    for h in range(HEADS // 2, HEADS):
        inner_hq = closing(h, lane, lane1, b_all, x_ref, gy, dxs, hbuf, qbuf, qcol, scale, skip_ref, gi_ref, inner_hq)

    step_grad = u_col + fade * qcol[...]
    gs_ref[...] = step_grad
    at_end = jnp.sum(scale * qcol[...], axis=0, keepdims=True) + exp_end * inner_hq
    gd_ref[...] = exact(upper, dcol[...] - dt * step_grad, NN) + at_end

    finish(gcs, gc_ref, ac_s, ac_r)
    finish(gbs, gb_ref, ab_s, ab_r)

    for copy in sent:
        copy.wait_send()

    @pl.when(odd == 1)
    def _():
        to_other.wait_send()
        for stage in range(2):
            for way, x_at in pairs:
                z_hop(way, stage, x_at, 1).wait_send()

    @pl.when(odd == 0)
    def _():
        for stage in range(2):
            for way, x_at in pairs:
                z_hop(way, stage, x_at, 0).wait_send()


def closing(h, lane, lane1, b_all, x_ref, gy, dxs, hbuf, qbuf, qcol, scale, skip_ref, gi_ref, inner_hq):
    ch = slice(h * WIDTH, (h + 1) * WIDTH)
    grad = qbuf[2 * h : 2 * h + 2].reshape(WIDTH, STATE)
    part, rest = split(grad)
    fed = mm(b_all, part, NT) + mm(b_all, rest, NT)
    met = jnp.sum(x_ref[:, ch].astype(F32) * fed, axis=1, keepdims=True)
    qcol[...] += jnp.where(lane == h, met, 0.0)
    gi_ref[:, ch] = (
        dxs[:, ch]
        + skip_ref[:, h : h + 1] * gy[:, ch].astype(F32)
        + scale[:, h : h + 1] * fed
    ).astype(BF16)
    state = hbuf[2 * h : 2 * h + 2].reshape(WIDTH, STATE)
    prod = state * grad
    total = jnp.sum(jnp.sum(prod, axis=0, keepdims=True), axis=1, keepdims=True)
    return inner_hq + jnp.where(lane1 == h, total, 0.0)


def local(grad_out, out_weight, ssm_input, step_size, log_decay, b_in, c_in, skip):
    vmem = pl.BlockSpec(memory_space=pltpu.VMEM)
    dma = pltpu.SemaphoreType.DMA
    slices = pltpu.VMEM((GROUP, SLICE, STATE), F32)
    parts = pltpu.VMEM((GROUP, PART, STATE), F32)
    square = pltpu.VMEM((TOK, STATE), F32)
    by_head = pltpu.VMEM((TOK, HEADS), F32)
    wide = pltpu.VMEM((TOK, ROWS), BF16)
    peers = dma((GROUP,))
    return pl.pallas_call(
        kernel,
        out_shape=(
            jax.ShapeDtypeStruct((TOK, ROWS), BF16),
            jax.ShapeDtypeStruct((TOK, HEADS), F32),
            jax.ShapeDtypeStruct((TOK, HEADS), F32),
            jax.ShapeDtypeStruct((TOK, STATE), F32),
            jax.ShapeDtypeStruct((TOK, STATE), F32),
        ),
        in_specs=[vmem] * 8,
        out_specs=[vmem] * 5,
        scratch_shapes=[
            pltpu.VMEM((8, ROWS, COLS), BF16),
            pltpu.VMEM((8, 2, TOK, COLS), BF16),
            pltpu.VMEM((2 * TOK, ROWS), F32),
            pltpu.VMEM((TOK, ROWS), F32),
            wide,
            wide,
            wide,
            pltpu.VMEM((TOK, ROWS), F32),
            pltpu.VMEM((TOK, TOK), F32),
            pltpu.VMEM((TOK, TOK), F32),
            pltpu.VMEM((HEADS, TOK), F32),
            by_head,
            by_head,
            pltpu.VMEM((HEADS, 8, 128), F32),
            pltpu.VMEM((GROUP, 8, 128), F32),
            slices, slices, slices, slices,
            slices, slices, slices, slices,
            square, square,
            parts, parts,
            square, square,
            dma((len(HOPS),)), dma((len(HOPS),)),
            dma((2,)), dma((3,)),
            dma((2, 2, 2)), dma((2, 2, 2)),
            dma((1,)), dma((1,)),
        ] + [peers] * 18,
        compiler_params=pltpu.CompilerParams(
            collective_id=0, has_side_effects=True, vmem_limit_bytes=52 * 2**20
        ),
        name="layer_backward",
    )(grad_out, out_weight, ssm_input, step_size, log_decay, b_in, c_in, skip.reshape(1, HEADS))


def solution(mesh):
    in_specs = (
        P("seq", "head"),
        P("head", "seq"),
        P("seq", "head"),
        P("seq", "head"),
        P("seq", "head"),
        P("seq", None),
        P("seq", None),
        P("head"),
    )
    out_specs = (
        P("seq", "head"),
        P("seq", "head"),
        P("seq", "head"),
        P("seq", None),
        P("seq", None),
    )
    return jax.shard_map(local, mesh=mesh, in_specs=in_specs, out_specs=out_specs, check_vma=False)
```

time: 650 us -> 165 us (0.25); the launches traced: 640 us -> 163 us
  waiting for transfers between devices: 539 us -> 0 us
  Pallas kernels: 0 us -> 154 us
  other arithmetic: 29.9 us -> 0 us
  matrix products: 28.5 us -> 0 us
  blocking collectives: 19.7 us -> 0 us
  between operations: 14 us -> 0.7 us
    all_gather x4 -> x0, waiting for transfers between devices: 397 us -> none  [the longest x2 192 us: entering(): gathered = jax.tree.map(lambda a: lax.all_gather(a, axis), part)]
    pallas_call x0 -> x1, Pallas kernels: none -> 154 us  [local(): pl.pallas_call(kernel, out_shape=(jax.ShapeDtypeStruct((TOK, ROWS), BF16)...]
    psum x1 -> x0, waiting for transfers between devices: 141 us -> none  [local(): grad_b, grad_c = lax.psum((gradients[3], gradients[4]), 'head')]
    dot_general x12 -> x0, matrix products: 28.5 us -> none  [the longest x1 11.6 us: local(): lax.dot_general(full_grad, lax.all_gather(out_weight, 'seq', axis=1, tile...]
    add x15 -> x0, other arithmetic: 23 us -> none  [compose(): second_part[0][:, None, None] * first_part[1] + second_part[1]]
    all_gather x1 -> x0, blocking collectives: 19.7 us -> none  [entering(): gathered = jax.tree.map(lambda a: lax.all_gather(a, axis), part)]
  transfers between devices with their start and end apart: 5 -> 0, of which waited for: 5 -> 0; matrix products, arithmetic and copies ran while one was open for 3% -> 0% of each run, Pallas kernels for 0% -> 0%
where the time goes in v1:
time: 165 us; the launch traced here: 163 us
  Pallas kernels  154 us (93%)
  local copies, waits for them, and re-layouts  8.11 us (5%)
    pallas_call x1, Pallas kernels, local(): pl.pallas_call(kernel, out_shape=(jax.ShapeDtypeStruct((TOK, ROWS), BF16)...  154 us
    unnamed x13, local copies, waits for them, and re-layouts  6.77 us

profile of v1, /device:TPU:1, one launch (start us, length us, event | category | flops | bytes accessed | tf_op | source)
XLA Modules:
  0.0 162.8 jit_solution(7073443772551027949)
XLA Ops:
  0.6 0.0 copy-start
  0.6 0.9 copy.13.dt_ref
  1.5 0.0 copy-start.3
  1.5 0.8 copy.14.ld_ref
  2.4 0.0 copy-done
  2.4 0.0 copy-done.3
  2.4 0.0 copy-start.1
  2.4 0.9 copy-done.1
  3.3 0.0 copy-start.2
  3.3 0.9 copy-done.2
  4.2 154.0 %layer_backward.1 = (bf16[256,1024]{1,0:T(8,128)(2,1)}, f32[256,8]{1,0:T(8,128)S(1)}, f32[256,8]{1,0:T(8,128)S(1)}, f32[256,256]{1,0:T(8,128)S(1)}, f32[256,256]{1,0:T(8,128)S(1)}) custom-call(bf16[256,512]{1,0:T(8,128)(2,1)S(1)} %copy-done, bf16[1024,512]{1,0:T(8,128)(2,1)} %w_ref.1, bf16[256,1024]{1,0:T(8,128)(2,1)} %x_ref.1, f32[256,8]{1,0:T(8,128)S(1)} %copy.13.dt_ref, ...), custom_call_target="tpu_custom_call" | custom-call | tf_op jit(solution)/shard_map/layer_backward/pallas_call | solution.py:474
  158.2 0.7 copy.15
  158.8 0.7 copy.16
  159.5 1.9 %copy.20 = bf16[256,1024]{1,0:T(8,128)(2,1)} copy(bf16[256,1024]{1,0:T(8,128)(2,1)} %get-tuple-element.15) | data formatting | bytes 1048576
  161.4 0.7 copy.21
  162.1 0.7 copy.22
Async XLA Ops:
  0.6 1.7 %copy-start = (bf16[256,512]{1,0:T(8,128)(2,1)S(1)}, bf16[256,512]{1,0:T(8,128)(2,1)}, u32[]{:S(2)}) copy-start(bf16[256,512]{1,0:T(8,128)(2,1)} %go_ref.1) | copy-start | bytes 786436
  1.5 0.9 copy-start.3
  2.4 0.9 copy-start.1
  3.3 0.9 copy-start.2

commit v2 on v1

v2 whole, which is shorter than its diff:
```python
import jax
import jax.numpy as jnp
from jax import lax
from jax.experimental import pallas as pl
from jax.experimental.pallas import tpu as pltpu
from jax.sharding import PartitionSpec as P

F32, BF16 = jnp.float32, jnp.bfloat16
HIGH = lax.Precision.HIGHEST
NN = (((1,), (0,)), ((), ()))
NT = (((1,), (1,)), ((), ()))
TN = (((0,), (0,)), ((), ()))

TOK = 256
HEADS = 8
WIDTH = 128
STATE = 256
ROWS = HEADS * WIDTH
COLS = 512
GROUP = 16
CHIPS = 8
SLICE = ROWS // GROUP
PART = TOK // GROUP
HALF = ROWS // 2
CHUNKS = 4
WIDE = ROWS // CHUNKS


def mm(a, b, dims):
    return lax.dot_general(a, b, dims, preferred_element_type=F32)


def exact(a, b, dims):
    return lax.dot_general(a, b, dims, precision=HIGH, preferred_element_type=F32)


def split(a):
    high = a.astype(BF16)
    return high, (a - high.astype(F32)).astype(BF16)


def remote(src, dst, send_sem, recv_sem, seq, head):
    return pltpu.make_async_remote_copy(
        src_ref=src,
        dst_ref=dst,
        send_sem=send_sem,
        recv_sem=recv_sem,
        device_id={"seq": seq, "head": head},
        device_id_type=pl.DeviceIdType.MESH,
    )


HOPS = {
    "u0": (0, 0, "up"),
    "d1": (0, HALF, "down"),
    "u1": (0, HALF, "up"),
    "d0": (0, 0, "down"),
    "f0": (-1, 0, "up"),
    "f1": (1, HALF, "down"),
}
HOP_AT = {name: at for at, name in enumerate(HOPS)}


def kernel(
    go_hbm, w_hbm, x_hbm, dt_hbm, ld_hbm, b_hbm, c_hbm, skip_hbm,
    gi_ref, gs_ref, gd_ref, gb_ref, gc_ref,
    x_ref, dt_ref, ld_ref, b_ref, c_ref, skip_ref, in_s,
    wbuf, gbuf, accp, acco, pbufp, pbufo, xout, xin, gy, ge, xs, xs_low, wts, dxs, cb, vsum, urow, dcol, qcol, dtile, dother,
    sfw, hin, hpair, rfw, ofw, hback, hsend, hbuf,
    sbw, qin, qpair, rbw, obw, qback, qsend, qbuf, dcp, dbp, prc, prb, gcs, gbs,
    w_s, w_r, g_s, g_r, z_s, z_r, p_s, p_r, o_s, o_r, x_s, x_r, e_s, e_r, f_s, f_r, h_s, h_r, l_s, l_r, q_s, q_r,
    rc_s, rc_r, ac_s, ac_r, rb_s, rb_r, ab_s, ab_r,
):
    seq = lax.axis_index("seq")
    head = lax.axis_index("head")
    xh = lax.div(seq, 8)
    yy = lax.rem(lax.div(seq, 2), 4)
    core = lax.rem(seq, 2)
    xl = lax.div(head, 8)
    zz = lax.rem(head, 8)
    other = seq + 1 - 2 * core
    beside = (1 - xl) * 8 + zz
    home = lax.rem(zz, 2)
    odd = lax.rem(zz + core, 2)

    own_w = pltpu.make_async_copy(w_hbm, wbuf.at[yy], in_s.at[6])
    own_w.start()
    loads = [
        pltpu.make_async_copy(src, dst, in_s.at[i])
        for i, (src, dst) in enumerate(
            (
                (ld_hbm, ld_ref),
                (dt_hbm, dt_ref),
                (x_hbm, x_ref),
                (b_hbm, b_ref),
                (c_hbm, c_ref),
                (skip_hbm, skip_ref),
            )
        )
    ]
    for load in loads:
        load.start()

    barrier = pltpu.get_barrier_semaphore()

    def greet(s, h):
        pl.semaphore_signal(
            barrier, inc=1, device_id={"seq": s, "head": h}, device_id_type=pl.DeviceIdType.MESH
        )

    over = seq + 8 - 16 * xh
    over_other = other + 8 - 16 * xh
    for h in (beside, head):
        greet(other, h)
        greet(over_other, h)
    greet(over, beside)
    for d in range(1, CHIPS):
        greet(lax.rem(seq + 2 * d, GROUP), head)
    for d in range(1, GROUP):
        greet(seq, lax.rem(head + d, GROUP))
    pl.semaphore_wait(barrier, 5 + CHIPS - 1 + GROUP - 1)

    sent = []

    def start(copy):
        copy.start()
        sent.append(copy)

    go_seq = xl * 8 + yy * 2 + home
    go_slot = gbuf.at[xh * 4 + lax.div(zz, 2), core]
    stays = jnp.logical_and(xl == xh, core == home)
    start(remote(go_hbm, go_slot, g_s.at[0], g_r.at[xh, core], go_seq, beside))
    inside = remote(go_hbm, go_slot, g_s.at[1], g_r.at[xh, core], go_seq, head)
    at_home = pltpu.make_async_copy(go_hbm, go_slot, g_s.at[2])

    @pl.when(jnp.logical_not(stays))
    def _():
        inside.start()

    @pl.when(stays)
    def _():
        at_home.start()

    def hop(name):
        dy, row, way = HOPS[name]
        at = HOP_AT[name]
        where = pl.ds(row, HALF)
        slot = wbuf.at[lax.rem(yy + dy + 4, 4), where]
        src = w_hbm.at[where] if dy == 0 else slot
        to = xh * 8 + lax.rem(yy + (1 if way == "up" else 3), 4) * 2 + core
        return remote(src, slot, w_s.at[at], w_r.at[at], to, head)

    def go(*names):
        for name in names:
            start(hop(name))

    def got(*names):
        for name in names:
            dy, row, way = HOPS[name]
            at = HOP_AT[name]
            dy = dy - 1 if way == "up" else dy + 1
            slot = wbuf.at[lax.rem(yy + dy + 4, 4), pl.ds(row, HALF)]
            remote(slot, slot, w_s.at[at], w_r.at[at], seq, head).wait_recv()

    go("u0", "d1", "u1", "d0")

    def group_at(group):
        return (1 - xh if group == 0 else xh) * 4

    def go_got(group):
        half_at = 1 - xh if group == 0 else xh
        for tok in (1 - core, core):
            slot = gbuf.at[group_at(group) + lax.div(zz, 2), tok]
            came = remote(slot, slot, g_s.at[0], g_r.at[half_at, tok], seq, head)
            if group == 1 and tok is core:

                @pl.when(stays)
                def _():
                    at_home.wait()

                @pl.when(jnp.logical_not(stays))
                def _():
                    came.wait_recv()

            else:
                came.wait_recv()

    def unit(group, way, d, half):
        z_from = lax.rem(zz + (8 - d if way == 0 else d), 8)
        k = group_at(group) + lax.div(z_from, 2)
        return gbuf.at[k, way] if half else gbuf.at[k]

    def z_hop(way, stage, group, is_odd):
        part = unit(group, way, 2 * stage + is_odd, is_odd and stage == 1)
        z_to = lax.rem(zz + (1 if way == 0 else 7), 8)
        return remote(
            part, part, z_s.at[way, stage, group], z_r.at[way, stage, group], seq, xl * 8 + z_to
        )

    def z_got(way, stage, group, is_odd):
        part = unit(group, way, 2 * stage + (1 if is_odd else 2), (not is_odd) and stage == 1)
        remote(
            part, part, z_s.at[way, stage, group], z_r.at[way, stage, group], seq, head
        ).wait_recv()

    def z_pass(stage_in, stage_out, group, is_odd):
        for way in range(2):
            z_got(way, stage_in, group, is_odd)
            if stage_out is not None:
                z_hop(way, stage_out, group, is_odd).start()

    rows_i = lax.broadcasted_iota(jnp.int32, (TOK, TOK), 0)
    cols_i = lax.broadcasted_iota(jnp.int32, (TOK, TOK), 1)
    causal = rows_i >= cols_i
    lower = jnp.where(causal, 1.0, 0.0).astype(F32)
    upper = jnp.where(rows_i <= cols_i, 1.0, 0.0).astype(F32)
    eye = jnp.where(rows_i == cols_i, 1.0, 0.0).astype(F32)
    lane = lax.broadcasted_iota(jnp.int32, (TOK, HEADS), 1)
    lane1 = lax.broadcasted_iota(jnp.int32, (HEADS, 1), 0)
    for load in loads:
        load.wait()
    dt_row = dt_ref[...]
    ld = ld_ref[...]
    run = exact(lower, ld, NT)
    run_row = exact(ld, upper, NN)
    dt = exact(eye, dt_row, NT)
    end = run[TOK - 1 : TOK, :]
    fade = jnp.exp(end - run)
    scale = dt * fade
    rise = jnp.exp(run)
    exp_end = jnp.exp(end)

    @pl.when(odd == 0)
    def _():
        for group in range(2):
            go_got(group)
            for way in range(2):
                z_hop(way, 0, group, 0).start()

    b_all = b_ref[...]
    c_all = c_ref[...]
    for h in range(HEADS):
        ch = slice(h * WIDTH, (h + 1) * WIDTH)
        scaled = x_ref[:, ch].astype(F32) * scale[:, h : h + 1]
        part, rest = split(scaled)
        xs[:, ch] = part
        xs_low[:, ch] = rest
        made = mm(part, b_all, TN) + mm(rest, b_all, TN)
        sfw[2 * h : 2 * h + 2] = made.reshape(2, SLICE, STATE)
        dtile[h] = jnp.broadcast_to(exp_end[:, h : h + 1], (8, 128))

    chip = lax.div(seq, 2)

    def tile(table, q):
        return table[core * (HEADS // 2) + q // 2, 0:1, 0:1]

    def pair_up(own, got_half, pair, first):
        for q in range(CHIPS):
            keep = jnp.where(first, tile(dother, q), 1.0)
            take = jnp.where(first, 1.0, tile(dtile, q))
            pair[q, 0:SLICE] = keep * own[core * CHIPS + q] + take * got_half[q]

    def pair_apart(back, own, got_half, send, out, first):
        for q in range(CHIPS):
            enters = back[q]
            mine = jnp.where(first, 1.0, tile(dother, q))
            here = jnp.where(first, 0.0, 1.0)
            out[core * CHIPS + q] = mine * enters + here * got_half[q]
            theirs = jnp.where(first, tile(dtile, q), 1.0)
            there = jnp.where(first, 1.0, 0.0)
            send[q] = theirs * enters + there * own[core * CHIPS + q]

    def half_of(buf, which):
        return buf.at[pl.ds(pl.multiple_of(which * CHIPS, CHIPS), CHIPS)]

    def to_chips(src, dst, ss, rs):
        for d in range(1, CHIPS):
            peer = lax.rem(chip + d, CHIPS)
            start(remote(src.at[peer], dst.at[chip], ss.at[d], rs.at[d], peer * 2 + core, head))
        dst[chip] = src[chip]

    def from_chips(dst, ss, rs):
        for d in range(1, CHIPS):
            peer = lax.rem(chip + CHIPS - d, CHIPS)
            remote(dst.at[peer], dst.at[peer], ss.at[d], rs.at[d], seq, head).wait_recv()

    first_fw = core == 0
    first_bw = core == 1
    tiles = remote(dtile, dother, e_s.at[0], e_r.at[0], other, head)
    start(tiles)
    halves = remote(half_of(sfw, 1 - core), hin, e_s.at[1], e_r.at[1], other, head)
    start(halves)

    cb[...] = mm(c_all, b_all, NT)
    got("u0")
    go("f0")
    got("d1")
    go("f1")

    tiles.wait_recv()
    halves.wait_recv()
    pair_up(sfw, hin, hpair, first_fw)
    for q in range(CHIPS):
        both = tile(dtile, q) * tile(dother, q)
        hpair[q, SLICE : SLICE + 8] = jnp.broadcast_to(both, (8, STATE))

    @pl.when(odd == 1)
    def _():
        z_pass(0, 0, 0, 1)
        z_pass(0, 0, 1, 1)
        z_pass(1, 1, 0, 1)

    @pl.when(odd == 0)
    def _():
        z_pass(0, 1, 0, 0)
        z_pass(0, 1, 1, 0)
        z_pass(1, None, 0, 0)

    def scan(order, inbox, outbox):
        state = jnp.zeros((SLICE, STATE), F32)
        for q in order:
            outbox[q] = state
            state = state * rfw[q, SLICE : SLICE + 1, :] + inbox[q, 0:SLICE]

    def product(group, acc, n):
        total = None
        for k in range(4):
            left = gbuf[group_at(group) + k].reshape(2 * TOK, COLS)
            new = mm(left, wbuf[k, n * WIDE : (n + 1) * WIDE, :], NT)
            total = new if total is None else total + new
        acc[n] = total.reshape(2, TOK, WIDE)

    own_w.wait()
    got("u1", "d0", "f0", "f1")
    swaps = []
    for n in range(CHUNKS):
        product(0, accp, n)
        swap = remote(accp.at[n, 1 - core], pbufp.at[n], p_s.at[n], p_r.at[n], other, head)
        start(swap)
        swaps.append(swap)
    crossings = []
    for n in range(CHUNKS):
        swaps[n].wait_recv()
        xout[n] = (accp[n, core] + pbufp[n]).astype(BF16)
        cross = remote(xout.at[n], xin.at[n], x_s.at[n], x_r.at[n], over, head)
        start(cross)
        crossings.append(cross)
    to_chips(hpair, rfw, f_s, f_r)

    @pl.when(odd == 1)
    def _():
        z_pass(1, 1, 1, 1)

    @pl.when(odd == 0)
    def _():
        z_pass(1, None, 1, 0)

    swaps = []
    for n in range(CHUNKS):
        product(1, acco, n)
        swap = remote(acco.at[n, 1 - core], pbufo.at[n], o_s.at[n], o_r.at[n], other, head)
        start(swap)
        swaps.append(swap)
    from_chips(rfw, f_s, f_r)
    scan(range(CHIPS), rfw, ofw)
    to_chips(ofw, hback, h_s, h_r)
    for n in range(CHUNKS):
        swaps[n].wait_recv()
        acco[n, core] = acco[n, core] + pbufo[n]

    for h in range(HEADS):
        ch = slice(h * WIDTH, (h + 1) * WIDTH)
        n, at = h // 2, slice((h % 2) * WIDTH, (h % 2 + 1) * WIDTH)
        if h % 2 == 0:
            crossings[n].wait_recv()
        up = (acco[n, core][:, at] + xin[n][:, at].astype(F32)).astype(BF16)
        gy[:, ch] = up
        part, rest = split(up.astype(F32) * rise[:, h : h + 1])
        ge[:, ch] = part
        made = mm(part, c_all, TN) + mm(rest, c_all, TN)
        sbw[2 * h : 2 * h + 2] = made.reshape(2, SLICE, STATE)
    q_halves = remote(half_of(sbw, 1 - core), qin, e_s.at[3], e_r.at[3], other, head)
    start(q_halves)
    q_halves.wait_recv()
    pair_up(sbw, qin, qpair, first_bw)
    to_chips(qpair, rbw, l_s, l_r)
    from_chips(hback, h_s, h_r)
    pair_apart(hback, sfw, hin, hsend, hbuf, first_fw)
    h_swap = remote(hsend, half_of(hbuf, core), e_s.at[2], e_r.at[2], other, head)
    start(h_swap)

    vsum[...] = jnp.zeros((TOK, TOK), F32)
    dcol[...] = jnp.zeros((TOK, HEADS), F32)

    def inner(h):
        ch = slice(h * WIDTH, (h + 1) * WIDTH)
        weights = wts.at[h % 2]
        u_sum = [jnp.zeros((1, WIDTH), F32), jnp.zeros((1, TOK - WIDTH), F32)]
        for r in range(4):
            rows = slice(r * 64, (r + 1) * 64)
            wide = WIDTH if r < 2 else TOK
            gx = mm(gy[rows, ch], x_ref[:wide, ch], NT)
            gaps = run[rows, h : h + 1] - run_row[h : h + 1, :wide]
            decay = jnp.exp(jnp.where(causal[rows, :wide], gaps, -1e30))
            steps = dt_row[h : h + 1, :wide]
            mixed = decay * cb[rows, :wide]
            both = mixed * gx
            vsum[rows, :wide] += decay * gx * steps
            weights[rows, :wide] = (mixed * steps).astype(BF16)
            down = jnp.sum(both, axis=0, keepdims=True)
            u_sum[0] += down[:, :WIDTH]
            if r >= 2:
                u_sum[1] += down[:, WIDTH:]
            along = jnp.sum(both * steps, axis=1, keepdims=True)
            dcol[rows, :] += jnp.where(lane[rows] == h, along, 0.0)
        urow[h : h + 1, :WIDTH] = u_sum[0]
        urow[h : h + 1, WIDTH:] = u_sum[1]
        dxs[:WIDTH, ch] = mm(weights[:, :WIDTH], gy[:, ch], TN)
        dxs[WIDTH:, ch] = mm(weights[WIDTH:, WIDTH:], gy[WIDTH:, ch], TN)

    def inner_read(h):
        ch = slice(h * WIDTH, (h + 1) * WIDTH)
        part, rest = split(hbuf[2 * h : 2 * h + 2].reshape(WIDTH, STATE))
        read = mm(c_all, part, NT) + mm(c_all, rest, NT)
        along = rise[:, h : h + 1] * jnp.sum(gy[:, ch].astype(F32) * read, axis=1, keepdims=True)
        dcol[...] += jnp.where(lane == h, along, 0.0)

    for h in range(HEADS):
        inner(h)
    half = half_of(hbuf, 1 - core)
    remote(half, half, e_s.at[2], e_r.at[2], other, head).wait_recv()

    from_chips(rbw, l_s, l_r)
    scan(range(CHIPS - 1, -1, -1), rbw, obw)
    to_chips(obw, qback, q_s, q_r)

    for h in range(HEADS):
        inner_read(h)
    v_hi = vsum[...].astype(BF16)
    v_lo = (vsum[...] - v_hi.astype(F32)).astype(BF16)

    def spread(src, dst, ss, rs):
        for d in range(1, GROUP):
            peer = lax.rem(head + d, GROUP)
            part = src.at[pl.ds(pl.multiple_of(peer * PART, PART), PART)]
            start(remote(part, dst.at[head], ss.at[d], rs.at[d], seq, peer))
        dst[head] = src[pl.ds(pl.multiple_of(head * PART, PART), PART)]

    def collect(inbox, whole, ss, rs, ss2, rs2):
        for d in range(1, GROUP):
            peer = lax.rem(head + GROUP - d, GROUP)
            remote(inbox.at[peer], inbox.at[peer], ss.at[d], rs.at[d], seq, head).wait_recv()
        total = inbox[0].astype(F32)
        for i in range(1, GROUP):
            total = total + inbox[i].astype(F32)
        own = pl.ds(pl.multiple_of(head * PART, PART), PART)
        whole[own] = total.astype(whole.dtype)
        for d in range(1, GROUP):
            peer = lax.rem(head + d, GROUP)
            start(remote(whole.at[own], whole.at[own], ss2.at[d], rs2.at[d], seq, peer))

    def finish(whole, out, ss, rs):
        for d in range(1, GROUP):
            peer = lax.rem(head + GROUP - d, GROUP)
            part = whole.at[pl.ds(pl.multiple_of(peer * PART, PART), PART)]
            remote(part, part, ss.at[d], rs.at[d], seq, head).wait_recv()
        out[...] = whole[...].astype(F32)

    dcp[...] = (
        mm(v_hi, b_all, NN)
        + mm(v_lo, b_all, NN)
        + mm(ge[...], hbuf[...].reshape(ROWS, STATE).astype(BF16), NN)
    )
    spread(dcp, prc, rc_s, rc_r)
    collect(prc, gcs, rc_s, rc_r, ac_s, ac_r)

    from_chips(qback, q_s, q_r)
    pair_apart(qback, sbw, qin, qsend, qbuf, first_bw)
    q_swap = remote(qsend, half_of(qbuf, core), e_s.at[4], e_r.at[4], other, head)
    start(q_swap)
    half = half_of(qbuf, 1 - core)
    remote(half, half, e_s.at[4], e_r.at[4], other, head).wait_recv()
    part, rest = split(qbuf[...].reshape(ROWS, STATE))
    db = mm(v_hi, c_all, TN) + mm(v_lo, c_all, TN)
    db += mm(xs[...], part, NN) + mm(xs_low[...], part, NN) + mm(xs[...], rest, NN)
    dbp[...] = db.astype(BF16)
    spread(dbp, prb, rb_s, rb_r)

    qcol[...] = jnp.zeros((TOK, HEADS), F32)
    inner_hq = jnp.zeros((HEADS, 1), F32)
    for h in range(HEADS // 2):
        inner_hq = closing(h, lane, lane1, b_all, x_ref, gy, dxs, hbuf, qbuf, qcol, scale, skip_ref, gi_ref, inner_hq)
    collect(prb, gbs, rb_s, rb_r, ab_s, ab_r)
    for h in range(HEADS // 2, HEADS):
        inner_hq = closing(h, lane, lane1, b_all, x_ref, gy, dxs, hbuf, qbuf, qcol, scale, skip_ref, gi_ref, inner_hq)

    step_grad = urow[...] + exact(fade * qcol[...], eye, TN)
    gs_ref[...] = step_grad
    at_end = jnp.sum(exact(scale * qcol[...], eye, TN), axis=1, keepdims=True)
    at_end += jnp.exp(run_row[:, TOK - 1 : TOK]) * inner_hq
    gd_ref[...] = exact(exact(dcol[...], eye, TN) - dt_row * step_grad, lower, NN) + at_end

    finish(gcs, gc_ref, ac_s, ac_r)
    finish(gbs, gb_ref, ab_s, ab_r)

    for copy in sent:
        copy.wait_send()

    @pl.when(jnp.logical_not(stays))
    def _():
        inside.wait_send()

    for is_odd in range(2):

        @pl.when(odd == is_odd)
        def _():
            for stage in range(2):
                for way in range(2):
                    for group in range(2):
                        z_hop(way, stage, group, is_odd).wait_send()


def closing(h, lane, lane1, b_all, x_ref, gy, dxs, hbuf, qbuf, qcol, scale, skip_ref, gi_ref, inner_hq):
    ch = slice(h * WIDTH, (h + 1) * WIDTH)
    grad = qbuf[2 * h : 2 * h + 2].reshape(WIDTH, STATE)
    part, rest = split(grad)
    fed = mm(b_all, part, NT) + mm(b_all, rest, NT)
    met = jnp.sum(x_ref[:, ch].astype(F32) * fed, axis=1, keepdims=True)
    qcol[...] += jnp.where(lane == h, met, 0.0)
    gi_ref[:, ch] = (
        dxs[:, ch]
        + skip_ref[:, h : h + 1] * gy[:, ch].astype(F32)
        + scale[:, h : h + 1] * fed
    ).astype(BF16)
    state = hbuf[2 * h : 2 * h + 2].reshape(WIDTH, STATE)
    prod = state * grad
    total = jnp.sum(jnp.sum(prod, axis=0, keepdims=True), axis=1, keepdims=True)
    return inner_hq + jnp.where(lane1 == h, total, 0.0)


def hand_over(*refs):
    given, out, room, sems = refs[:5], refs[5:10], refs[10:15], refs[15]
    come = [pltpu.make_async_copy(given[i], room[i], sems.at[i]) for i in range(5)]
    leave = [pltpu.make_async_copy(room[i], out[i], sems.at[5 + i]) for i in range(5)]
    for copy in come:
        copy.start()
    for i in range(5):
        come[i].wait()
        leave[i].start()
    for copy in leave:
        copy.wait()


def local(grad_out, out_weight, ssm_input, step_size, log_decay, b_in, c_in, skip):
    vmem = pl.BlockSpec(memory_space=pltpu.VMEM)
    here = pl.BlockSpec(memory_space=pl.ANY)
    dma = pltpu.SemaphoreType.DMA
    slices = pltpu.VMEM((GROUP, SLICE, STATE), F32)
    halves = pltpu.VMEM((CHIPS, SLICE, STATE), F32)
    tagged = pltpu.VMEM((CHIPS, SLICE + 8, STATE), F32)
    parts = pltpu.VMEM((GROUP, PART, STATE), F32)
    short_parts = pltpu.VMEM((GROUP, PART, STATE), BF16)
    short_square = pltpu.VMEM((TOK, STATE), BF16)
    square = pltpu.VMEM((TOK, STATE), F32)
    by_row = pltpu.VMEM((HEADS, TOK), F32)
    sums = pltpu.VMEM((CHUNKS, TOK, WIDE), F32)
    short = pltpu.VMEM((CHUNKS, TOK, WIDE), BF16)
    by_head = pltpu.VMEM((TOK, HEADS), F32)
    wide = pltpu.VMEM((TOK, ROWS), BF16)
    peers = dma((GROUP,))
    gi, gs, gd, gb, gc = pl.pallas_call(
        kernel,
        out_shape=(
            jax.ShapeDtypeStruct((TOK, ROWS), BF16),
            jax.ShapeDtypeStruct((HEADS, TOK), F32),
            jax.ShapeDtypeStruct((HEADS, TOK), F32),
            jax.ShapeDtypeStruct((TOK, STATE), F32),
            jax.ShapeDtypeStruct((TOK, STATE), F32),
        ),
        in_specs=[here] * 8,
        out_specs=[vmem] * 5,
        scratch_shapes=[
            wide,
            by_row, by_row,
            pltpu.VMEM((TOK, STATE), BF16), pltpu.VMEM((TOK, STATE), BF16),
            pltpu.VMEM((1, HEADS), F32),
            dma((7,)),
            pltpu.VMEM((4, ROWS, COLS), BF16),
            pltpu.VMEM((8, 2, TOK, COLS), BF16),
            pltpu.VMEM((CHUNKS, 2, TOK, WIDE), F32), pltpu.VMEM((CHUNKS, 2, TOK, WIDE), F32),
            sums, sums, short, short,
            wide,
            wide,
            wide, wide,
            pltpu.VMEM((2, TOK, TOK), BF16),
            pltpu.VMEM((TOK, ROWS), F32),
            pltpu.VMEM((TOK, TOK), F32),
            pltpu.VMEM((TOK, TOK), F32),
            pltpu.VMEM((HEADS, TOK), F32),
            by_head,
            by_head,
            pltpu.VMEM((HEADS, 8, 128), F32),
            pltpu.VMEM((HEADS, 8, 128), F32),
            slices, halves, tagged, tagged, halves, halves, halves, slices,
            slices, halves, halves, halves, halves, halves, halves, slices,
            square, short_square,
            parts, short_parts,
            square, short_square,
            dma((len(HOPS),)), dma((len(HOPS),)),
            dma((3,)), dma((2, 2)),
            dma((2, 2, 2)), dma((2, 2, 2)),
            dma((CHUNKS,)), dma((CHUNKS,)),
            dma((CHUNKS,)), dma((CHUNKS,)),
            dma((CHUNKS,)), dma((CHUNKS,)),
        ] + [peers] * 18,
        compiler_params=pltpu.CompilerParams(
            collective_id=0, has_side_effects=True, vmem_limit_bytes=60 * 2**20
        ),
        name="layer_backward",
    )(
        grad_out, out_weight, ssm_input, step_size.T, log_decay.T, b_in, c_in, skip.reshape(1, HEADS)
    )
    gi, gs, gd, gb, gc = pl.pallas_call(
        hand_over,
        out_shape=tuple(jax.ShapeDtypeStruct(a.shape, a.dtype) for a in (gi, gs, gd, gb, gc)),
        in_specs=[here] * 5,
        out_specs=[here] * 5,
        scratch_shapes=[pltpu.VMEM(a.shape, a.dtype) for a in (gi, gs, gd, gb, gc)] + [dma((10,))],
        name="hand_over",
    )(gi, gs, gd, gb, gc)
    return gi, gs.T, gd.T, gb, gc


def solution(mesh):
    in_specs = (
        P("seq", "head"),
        P("head", "seq"),
        P("seq", "head"),
        P("seq", "head"),
        P("seq", "head"),
        P("seq", None),
        P("seq", None),
        P("head"),
    )
    out_specs = (
        P("seq", "head"),
        P("seq", "head"),
        P("seq", "head"),
        P("seq", None),
        P("seq", None),
    )
    return jax.shard_map(local, mesh=mesh, in_specs=in_specs, out_specs=out_specs, check_vma=False)
```

time: 165 us -> 131 us (0.79); the launches traced: 163 us -> 131 us
  Pallas kernels: 154 us -> 130 us
  local copies, waits for them, and re-layouts: 8.11 us -> 0 us
    pallas_call x1, Pallas kernels: 154 us -> 128 us  [local(): pl.pallas_call(kernel, out_shape=(jax.ShapeDtypeStruct((TOK, ROWS), BF16)...]
    unnamed x13 -> x0, local copies, waits for them, and re-layouts: 6.77 us -> none
    pallas_call x0 -> x1, Pallas kernels: none -> 2.1 us  [local(): pl.pallas_call(hand_over, out_shape=tuple((jax.ShapeDtypeStruct(a.shape,...]
where the time goes in v2:
time: 131 us
  Pallas kernels  130 us (99%)
    pallas_call x1, Pallas kernels, local(): pl.pallas_call(kernel, out_shape=(jax.ShapeDtypeStruct((TOK, ROWS), BF16)...  128 us

profile of v2, /device:TPU:1, one launch (start us, length us, event | category | flops | bytes accessed | tf_op | source)
XLA Modules:
  0.0 130.8 jit_solution(7482926798463647372)
XLA Ops:
  0.6 127.9 %layer_backward.1 = (bf16[256,1024]{1,0:T(8,128)(2,1)}, f32[8,256]{1,0:T(8,128)}, f32[8,256]{1,0:T(8,128)}, f32[256,256]{1,0:T(8,128)}, f32[256,256]{1,0:T(8,128)}) custom-call(bf16[256,512]{1,0:T(8,128)(2,1)} %go_hbm.1, bf16[1024,512]{1,0:T(8,128)(2,1)} %w_hbm.1, bf16[256,1024]{1,0:T(8,128)(2,1)} %x_hbm.1, f32[8,256]{1,0:T(8,128)} %bitcast.5, ...), custom_call_target="tpu_custom_call" | custom-call | tf_op jit(solution)/shard_map/layer_backward/pallas_call | solution.py:571
  128.5 2.1 %hand_over.1 = (bf16[256,1024]{1,0:T(8,128)(2,1)}, f32[8,256]{1,0:T(8,128)}, f32[8,256]{1,0:T(8,128)}, f32[256,256]{1,0:T(8,128)}, f32[256,256]{1,0:T(8,128)}) custom-call(bf16[256,1024]{1,0:T(8,128)(2,1)} %get-tuple-element.15.refs_0_, f32[8,256]{1,0:T(8,128)} %get-tuple-element.16.refs_1_, f32[8,256]{1,0:T(8,128)} %get-tuple-element.17.refs_2_, ...), custom_call_target="tpu_custom_call" | custom-call | tf_op jit(solution)/shard_map/hand_over/pallas_call | solution.py:623

commit v3 on v2

--- a/solution.py
+++ b/solution.py
@@ -65,7 +65,7 @@
     go_hbm, w_hbm, x_hbm, dt_hbm, ld_hbm, b_hbm, c_hbm, skip_hbm,
     gi_ref, gs_ref, gd_ref, gb_ref, gc_ref,
     x_ref, dt_ref, ld_ref, b_ref, c_ref, skip_ref, in_s,
-    wbuf, gbuf, accp, acco, pbufp, pbufo, xout, xin, gy, ge, xs, xs_low, wts, dxs, cb, vsum, urow, dcol, qcol, dtile, dother,
+    wbuf, gbuf, accp, acco, pbufp, pbufo, xout, xin, gy, ge, ge_low, xs, xs_low, wts, dxs, cb, vsum, urow, dcol, qcol, dtile, dother,
     sfw, hin, hpair, rfw, ofw, hback, hsend, hbuf,
     sbw, qin, qpair, rbw, obw, qback, qsend, qbuf, dcp, dbp, prc, prb, gcs, gbs,
     w_s, w_r, g_s, g_r, z_s, z_r, p_s, p_r, o_s, o_r, x_s, x_r, e_s, e_r, f_s, f_r, h_s, h_r, l_s, l_r, q_s, q_r,
@@ -230,12 +230,14 @@
     rise = jnp.exp(run)
     exp_end = jnp.exp(end)
 
+    def z_begin(group):
+        go_got(group)
+        for way in range(2):
+            z_hop(way, 0, group, 0).start()
+
     @pl.when(odd == 0)
     def _():
-        for group in range(2):
-            go_got(group)
-            for way in range(2):
-                z_hop(way, 0, group, 0).start()
+        z_begin(0)
 
     b_all = b_ref[...]
     c_all = c_ref[...]
@@ -297,6 +299,10 @@
     got("d1")
     go("f1")
 
+    @pl.when(odd == 1)
+    def _():
+        z_pass(0, 0, 0, 1)
+
     tiles.wait_recv()
     halves.wait_recv()
     pair_up(sfw, hin, hpair, first_fw)
@@ -304,17 +310,20 @@
         both = tile(dtile, q) * tile(dother, q)
         hpair[q, SLICE : SLICE + 8] = jnp.broadcast_to(both, (8, STATE))
 
+    @pl.when(odd == 0)
+    def _():
+        z_pass(0, 1, 0, 0)
+        z_begin(1)
+
     @pl.when(odd == 1)
     def _():
-        z_pass(0, 0, 0, 1)
+        z_pass(1, 1, 0, 1)
         z_pass(0, 0, 1, 1)
-        z_pass(1, 1, 0, 1)
 
     @pl.when(odd == 0)
     def _():
-        z_pass(0, 1, 0, 0)
+        z_pass(1, None, 0, 0)
         z_pass(0, 1, 1, 0)
-        z_pass(1, None, 0, 0)
 
     def scan(order, inbox, outbox):
         state = jnp.zeros((SLICE, STATE), F32)
@@ -332,19 +341,24 @@
 
     own_w.wait()
     got("u1", "d0", "f0", "f1")
+    crossings = []
+
+    def cross_over(n):
+        swaps[n].wait_recv()
+        xout[n] = (accp[n, core] + pbufp[n]).astype(BF16)
+        cross = remote(xout.at[n], xin.at[n], x_s.at[n], x_r.at[n], over, head)
+        start(cross)
+        crossings.append(cross)
+
     swaps = []
     for n in range(CHUNKS):
         product(0, accp, n)
         swap = remote(accp.at[n, 1 - core], pbufp.at[n], p_s.at[n], p_r.at[n], other, head)
         start(swap)
         swaps.append(swap)
-    crossings = []
-    for n in range(CHUNKS):
-        swaps[n].wait_recv()
-        xout[n] = (accp[n, core] + pbufp[n]).astype(BF16)
-        cross = remote(xout.at[n], xin.at[n], x_s.at[n], x_r.at[n], over, head)
-        start(cross)
-        crossings.append(cross)
+        if n > 0:
+            cross_over(n - 1)
+    cross_over(CHUNKS - 1)
     to_chips(hpair, rfw, f_s, f_r)
 
     @pl.when(odd == 1)
@@ -377,6 +391,7 @@
         gy[:, ch] = up
         part, rest = split(up.astype(F32) * rise[:, h : h + 1])
         ge[:, ch] = part
+        ge_low[:, ch] = rest
         made = mm(part, c_all, TN) + mm(rest, c_all, TN)
         sbw[2 * h : 2 * h + 2] = made.reshape(2, SLICE, STATE)
     q_halves = remote(half_of(sbw, 1 - core), qin, e_s.at[3], e_r.at[3], other, head)
@@ -466,13 +481,11 @@
             remote(part, part, ss.at[d], rs.at[d], seq, head).wait_recv()
         out[...] = whole[...].astype(F32)
 
-    dcp[...] = (
-        mm(v_hi, b_all, NN)
-        + mm(v_lo, b_all, NN)
-        + mm(ge[...], hbuf[...].reshape(ROWS, STATE).astype(BF16), NN)
-    )
+    part, rest = split(hbuf[...].reshape(ROWS, STATE))
+    dc = mm(v_hi, b_all, NN) + mm(v_lo, b_all, NN)
+    dc += mm(ge[...], part, NN) + mm(ge_low[...], part, NN) + mm(ge[...], rest, NN)
+    dcp[...] = dc.astype(BF16)
     spread(dcp, prc, rc_s, rc_r)
-    collect(prc, gcs, rc_s, rc_r, ac_s, ac_r)
 
     from_chips(qback, q_s, q_r)
     pair_apart(qback, sbw, qin, qsend, qbuf, first_bw)
@@ -485,6 +498,7 @@
     db += mm(xs[...], part, NN) + mm(xs_low[...], part, NN) + mm(xs[...], rest, NN)
     dbp[...] = db.astype(BF16)
     spread(dbp, prb, rb_s, rb_r)
+    collect(prc, gcs, rc_s, rc_r, ac_s, ac_r)
 
     qcol[...] = jnp.zeros((TOK, HEADS), F32)
     inner_hq = jnp.zeros((HEADS, 1), F32)
@@ -558,10 +572,8 @@
     slices = pltpu.VMEM((GROUP, SLICE, STATE), F32)
     halves = pltpu.VMEM((CHIPS, SLICE, STATE), F32)
     tagged = pltpu.VMEM((CHIPS, SLICE + 8, STATE), F32)
-    parts = pltpu.VMEM((GROUP, PART, STATE), F32)
     short_parts = pltpu.VMEM((GROUP, PART, STATE), BF16)
     short_square = pltpu.VMEM((TOK, STATE), BF16)
-    square = pltpu.VMEM((TOK, STATE), F32)
     by_row = pltpu.VMEM((HEADS, TOK), F32)
     sums = pltpu.VMEM((CHUNKS, TOK, WIDE), F32)
     short = pltpu.VMEM((CHUNKS, TOK, WIDE), BF16)
@@ -590,7 +602,7 @@
             pltpu.VMEM((CHUNKS, 2, TOK, WIDE), F32), pltpu.VMEM((CHUNKS, 2, TOK, WIDE), F32),
             sums, sums, short, short,
             wide,
-            wide,
+            wide, wide,
             wide, wide,
             pltpu.VMEM((2, TOK, TOK), BF16),
             pltpu.VMEM((TOK, ROWS), F32),
@@ -603,9 +615,9 @@
             pltpu.VMEM((HEADS, 8, 128), F32),
             slices, halves, tagged, tagged, halves, halves, halves, slices,
             slices, halves, halves, halves, halves, halves, halves, slices,
-            square, short_square,
-            parts, short_parts,
-            square, short_square,
+            short_square, short_square,
+            short_parts, short_parts,
+            short_square, short_square,
             dma((len(HOPS),)), dma((len(HOPS),)),
             dma((3,)), dma((2, 2)),
             dma((2, 2, 2)), dma((2, 2, 2)),

time: 131 us -> 135 us (1.031)
  Pallas kernels: 130 us -> 134 us
    pallas_call x1, Pallas kernels: 128 us -> 132 us  [local(): pl.pallas_call(kernel, out_shape=(jax.ShapeDtypeStruct((TOK, ROWS), BF16)...]
where the time goes in v3:
time: 135 us
  Pallas kernels  134 us (99%)
    pallas_call x1, Pallas kernels, local(): pl.pallas_call(kernel, out_shape=(jax.ShapeDtypeStruct((TOK, ROWS), BF16)...  132 us

profile of v3, /device:TPU:1, one launch (start us, length us, event | category | flops | bytes accessed | tf_op | source)
XLA Modules:
  0.0 134.9 jit_solution(15816319441485314493)
XLA Ops:
  0.6 132.0 %layer_backward.1 = (bf16[256,1024]{1,0:T(8,128)(2,1)}, f32[8,256]{1,0:T(8,128)}, f32[8,256]{1,0:T(8,128)}, f32[256,256]{1,0:T(8,128)}, f32[256,256]{1,0:T(8,128)}) custom-call(bf16[256,512]{1,0:T(8,128)(2,1)} %go_hbm.1, bf16[1024,512]{1,0:T(8,128)(2,1)} %w_hbm.1, bf16[256,1024]{1,0:T(8,128)(2,1)} %x_hbm.1, f32[8,256]{1,0:T(8,128)} %bitcast.5, ...), custom_call_target="tpu_custom_call" | custom-call | tf_op jit(solution)/shard_map/layer_backward/pallas_call | solution.py:583
  132.6 2.1 %hand_over.1 = (bf16[256,1024]{1,0:T(8,128)(2,1)}, f32[8,256]{1,0:T(8,128)}, f32[8,256]{1,0:T(8,128)}, f32[256,256]{1,0:T(8,128)}, f32[256,256]{1,0:T(8,128)}) custom-call(bf16[256,1024]{1,0:T(8,128)(2,1)} %get-tuple-element.15.refs_0_, f32[8,256]{1,0:T(8,128)} %get-tuple-element.16.refs_1_, f32[8,256]{1,0:T(8,128)} %get-tuple-element.17.refs_2_, ...), custom_call_target="tpu_custom_call" | custom-call | tf_op jit(solution)/shard_map/hand_over/pallas_call | solution.py:635

commit v4 on v3

--- a/solution.py
+++ b/solution.py
@@ -323,7 +323,6 @@
     @pl.when(odd == 0)
     def _():
         z_pass(1, None, 0, 0)
-        z_pass(0, 1, 1, 0)
 
     def scan(order, inbox, outbox):
         state = jnp.zeros((SLICE, STATE), F32)
@@ -367,6 +366,7 @@
 
     @pl.when(odd == 0)
     def _():
+        z_pass(0, 1, 1, 0)
         z_pass(1, None, 1, 0)
 
     swaps = []

time: 135 us -> 126 us (0.933)
  Pallas kernels: 134 us -> 125 us
    pallas_call x1, Pallas kernels: 132 us -> 123 us  [local(): pl.pallas_call(kernel, out_shape=(jax.ShapeDtypeStruct((TOK, ROWS), BF16)...]
where the time goes in v4:
time: 126 us; the launch traced here: 125 us
  Pallas kernels  125 us (99%)
    pallas_call x1, Pallas kernels, local(): pl.pallas_call(kernel, out_shape=(jax.ShapeDtypeStruct((TOK, ROWS), BF16)...  123 us

profile of v4, /device:TPU:1, one launch (start us, length us, event | category | flops | bytes accessed | tf_op | source)
XLA Modules:
  0.0 125.5 jit_solution(3153240506951376583)
XLA Ops:
  0.6 122.6 %layer_backward.1 = (bf16[256,1024]{1,0:T(8,128)(2,1)}, f32[8,256]{1,0:T(8,128)}, f32[8,256]{1,0:T(8,128)}, f32[256,256]{1,0:T(8,128)}, f32[256,256]{1,0:T(8,128)}) custom-call(bf16[256,512]{1,0:T(8,128)(2,1)} %go_hbm.1, bf16[1024,512]{1,0:T(8,128)(2,1)} %w_hbm.1, bf16[256,1024]{1,0:T(8,128)(2,1)} %x_hbm.1, f32[8,256]{1,0:T(8,128)} %bitcast.5, ...), custom_call_target="tpu_custom_call" | custom-call | tf_op jit(solution)/shard_map/layer_backward/pallas_call | solution.py:583
  123.2 2.1 %hand_over.1 = (bf16[256,1024]{1,0:T(8,128)(2,1)}, f32[8,256]{1,0:T(8,128)}, f32[8,256]{1,0:T(8,128)}, f32[256,256]{1,0:T(8,128)}, f32[256,256]{1,0:T(8,128)}) custom-call(bf16[256,1024]{1,0:T(8,128)(2,1)} %get-tuple-element.15.refs_0_, f32[8,256]{1,0:T(8,128)} %get-tuple-element.16.refs_1_, f32[8,256]{1,0:T(8,128)} %get-tuple-element.17.refs_2_, ...), custom_call_target="tpu_custom_call" | custom-call | tf_op jit(solution)/shard_map/hand_over/pallas_call | solution.py:635

commit v5 on v4

--- a/solution.py
+++ b/solution.py
@@ -309,6 +309,7 @@
     for q in range(CHIPS):
         both = tile(dtile, q) * tile(dother, q)
         hpair[q, SLICE : SLICE + 8] = jnp.broadcast_to(both, (8, STATE))
+    to_chips(hpair, rfw, f_s, f_r)
 
     @pl.when(odd == 0)
     def _():
@@ -338,8 +339,11 @@
             total = new if total is None else total + new
         acc[n] = total.reshape(2, TOK, WIDE)
 
+    from_chips(rfw, f_s, f_r)
+    scan(range(CHIPS), rfw, ofw)
     own_w.wait()
     got("u1", "d0", "f0", "f1")
+    to_chips(ofw, hback, h_s, h_r)
     crossings = []
 
     def cross_over(n):
@@ -358,7 +362,6 @@
         if n > 0:
             cross_over(n - 1)
     cross_over(CHUNKS - 1)
-    to_chips(hpair, rfw, f_s, f_r)
 
     @pl.when(odd == 1)
     def _():
@@ -375,9 +378,6 @@
         swap = remote(acco.at[n, 1 - core], pbufo.at[n], o_s.at[n], o_r.at[n], other, head)
         start(swap)
         swaps.append(swap)
-    from_chips(rfw, f_s, f_r)
-    scan(range(CHIPS), rfw, ofw)
-    to_chips(ofw, hback, h_s, h_r)
     for n in range(CHUNKS):
         swaps[n].wait_recv()
         acco[n, core] = acco[n, core] + pbufo[n]

time: 126 us -> 131 us (1.040)
  Pallas kernels: 125 us -> 130 us
    pallas_call x1, Pallas kernels: 123 us -> 128 us  [local(): pl.pallas_call(kernel, out_shape=(jax.ShapeDtypeStruct((TOK, ROWS), BF16)...]
where the time goes in v5:
time: 131 us
  Pallas kernels  130 us (99%)
    pallas_call x1, Pallas kernels, local(): pl.pallas_call(kernel, out_shape=(jax.ShapeDtypeStruct((TOK, ROWS), BF16)...  128 us

profile of v5, /device:TPU:1, one launch (start us, length us, event | category | flops | bytes accessed | tf_op | source)
XLA Modules:
  0.0 130.6 jit_solution(3734387903744465457)
XLA Ops:
  0.6 127.7 %layer_backward.1 = (bf16[256,1024]{1,0:T(8,128)(2,1)}, f32[8,256]{1,0:T(8,128)}, f32[8,256]{1,0:T(8,128)}, f32[256,256]{1,0:T(8,128)}, f32[256,256]{1,0:T(8,128)}) custom-call(bf16[256,512]{1,0:T(8,128)(2,1)} %go_hbm.1, bf16[1024,512]{1,0:T(8,128)(2,1)} %w_hbm.1, bf16[256,1024]{1,0:T(8,128)(2,1)} %x_hbm.1, f32[8,256]{1,0:T(8,128)} %bitcast.5, ...), custom_call_target="tpu_custom_call" | custom-call | tf_op jit(solution)/shard_map/layer_backward/pallas_call | solution.py:583
  128.3 2.1 %hand_over.1 = (bf16[256,1024]{1,0:T(8,128)(2,1)}, f32[8,256]{1,0:T(8,128)}, f32[8,256]{1,0:T(8,128)}, f32[256,256]{1,0:T(8,128)}, f32[256,256]{1,0:T(8,128)}) custom-call(bf16[256,1024]{1,0:T(8,128)(2,1)} %get-tuple-element.15.refs_0_, f32[8,256]{1,0:T(8,128)} %get-tuple-element.16.refs_1_, f32[8,256]{1,0:T(8,128)} %get-tuple-element.17.refs_2_, ...), custom_call_target="tpu_custom_call" | custom-call | tf_op jit(solution)/shard_map/hand_over/pallas_call | solution.py:635

commit v6 on v4

--- a/solution.py
+++ b/solution.py
@@ -382,6 +382,11 @@
         swaps[n].wait_recv()
         acco[n, core] = acco[n, core] + pbufo[n]
 
+    def q_part(i):
+        part = pl.ds(pl.multiple_of((1 - core) * CHIPS + 4 * i, 4), 4)
+        at = 3 + 2 * i
+        return remote(sbw.at[part], qin.at[pl.ds(4 * i, 4)], e_s.at[at], e_r.at[at], other, head)
+
     for h in range(HEADS):
         ch = slice(h * WIDTH, (h + 1) * WIDTH)
         n, at = h // 2, slice((h % 2) * WIDTH, (h % 2 + 1) * WIDTH)
@@ -394,9 +399,14 @@
         ge_low[:, ch] = rest
         made = mm(part, c_all, TN) + mm(rest, c_all, TN)
         sbw[2 * h : 2 * h + 2] = made.reshape(2, SLICE, STATE)
-    q_halves = remote(half_of(sbw, 1 - core), qin, e_s.at[3], e_r.at[3], other, head)
-    start(q_halves)
-    q_halves.wait_recv()
+        if h % 2 == 1:
+
+            @pl.when(core == 1 - n // 2)
+            def _():
+                q_part(n % 2).start()
+
+    for i in range(2):
+        q_part(i).wait_recv()
     pair_up(sbw, qin, qpair, first_bw)
     to_chips(qpair, rbw, l_s, l_r)
     from_chips(hback, h_s, h_r)
@@ -486,16 +496,22 @@
     dc += mm(ge[...], part, NN) + mm(ge_low[...], part, NN) + mm(ge[...], rest, NN)
     dcp[...] = dc.astype(BF16)
     spread(dcp, prc, rc_s, rc_r)
+    db = mm(v_hi, c_all, TN) + mm(v_lo, c_all, TN)
 
     from_chips(qback, q_s, q_r)
     pair_apart(qback, sbw, qin, qsend, qbuf, first_bw)
     q_swap = remote(qsend, half_of(qbuf, core), e_s.at[4], e_r.at[4], other, head)
     start(q_swap)
+
+    def fed_by(which):
+        cols = pl.ds(pl.multiple_of(which * HALF, HALF), HALF)
+        part, rest = split(half_of(qbuf, which)[...].reshape(HALF, STATE))
+        return mm(xs[:, cols], part, NN) + mm(xs_low[:, cols], part, NN) + mm(xs[:, cols], rest, NN)
+
+    db += fed_by(core)
     half = half_of(qbuf, 1 - core)
     remote(half, half, e_s.at[4], e_r.at[4], other, head).wait_recv()
-    part, rest = split(qbuf[...].reshape(ROWS, STATE))
-    db = mm(v_hi, c_all, TN) + mm(v_lo, c_all, TN)
-    db += mm(xs[...], part, NN) + mm(xs_low[...], part, NN) + mm(xs[...], rest, NN)
+    db += fed_by(1 - core)
     dbp[...] = db.astype(BF16)
     spread(dbp, prb, rb_s, rb_r)
     collect(prc, gcs, rc_s, rc_r, ac_s, ac_r)
@@ -519,6 +535,8 @@
 
     for copy in sent:
         copy.wait_send()
+    for i in range(2):
+        q_part(i).wait_send()
 
     @pl.when(jnp.logical_not(stays))
     def _():

time: 126 us -> 125 us (level)
  no operation moved by 1% of the time
where the time goes in v6:
time: 125 us
  Pallas kernels  124 us (99%)
    pallas_call x1, Pallas kernels, local(): pl.pallas_call(kernel, out_shape=(jax.ShapeDtypeStruct((TOK, ROWS), BF16)...  122 us

profile of v6, /device:TPU:1, one launch (start us, length us, event | category | flops | bytes accessed | tf_op | source)
XLA Modules:
  0.0 125.2 jit_solution(12552257286722009655)
XLA Ops:
  0.6 122.3 %layer_backward.1 = (bf16[256,1024]{1,0:T(8,128)(2,1)}, f32[8,256]{1,0:T(8,128)}, f32[8,256]{1,0:T(8,128)}, f32[256,256]{1,0:T(8,128)}, f32[256,256]{1,0:T(8,128)}) custom-call(bf16[256,512]{1,0:T(8,128)(2,1)} %go_hbm.1, bf16[1024,512]{1,0:T(8,128)(2,1)} %w_hbm.1, bf16[256,1024]{1,0:T(8,128)(2,1)} %x_hbm.1, f32[8,256]{1,0:T(8,128)} %bitcast.5, ...), custom_call_target="tpu_custom_call" | custom-call | tf_op jit(solution)/shard_map/layer_backward/pallas_call | solution.py:601
  122.9 2.1 %hand_over.1 = (bf16[256,1024]{1,0:T(8,128)(2,1)}, f32[8,256]{1,0:T(8,128)}, f32[8,256]{1,0:T(8,128)}, f32[256,256]{1,0:T(8,128)}, f32[256,256]{1,0:T(8,128)}) custom-call(bf16[256,1024]{1,0:T(8,128)(2,1)} %get-tuple-element.15.refs_0_, f32[8,256]{1,0:T(8,128)} %get-tuple-element.16.refs_1_, f32[8,256]{1,0:T(8,128)} %get-tuple-element.17.refs_2_, ...), custom_call_target="tpu_custom_call" | custom-call | tf_op jit(solution)/shard_map/hand_over/pallas_call | solution.py:653
